TPU v7x, 32 devices: a whole 2x2x4 slice. The times are simulated.
32 devices in a mesh: groups: 2 (over y), seq: 16 (over z, x, core).
Axes of the slice: x: 2, y: 2, z: 4, core: 2. Of those that a mesh axis runs over, the one named last changes fastest.
Arguments:
- key_values: bfloat16 [3, 2048, 8192], P(None, 'seq', 'groups'), parts along dimension 2, may hold values from -14 to 14, as said below
- bases: bfloat16 [3, 2, 1024, 256], replicated, may hold values from -0.1875 to 0.1875
- owner_slots: int32 [3, 64], P(None, ('groups', 'seq')), parts along dimension 1, may hold values from 0 to 15, as said below
Outputs:
- received: bfloat16 [512, 512, 128], P(('groups', 'seq')), parts along dimension 0
- grams: float32 [6, 2, 256, 256], P('groups'), parts along dimension 0
- energies: float32 [6, 2, 1024], P('groups'), parts along dimension 0
There are 2 independent parts, one for each index of `groups`. A program takes and returns all parts, laid end to end along the dimension named above; an argument that names none is the same for every part. Nothing has to cross between parts.
Inputs may be any that keep to these rules, and one draw needn't show every extreme that they name: key_values are finite real values within the range. `owner_slots`: block j of a layer belongs to device j // 2 of seq; the 6 values of one device's blocks over all layers are distinct, so an owner's slot is written at most once; some owner has all 16 slots filled.
All inputs are finite; a program needn't handle non-finite values.
Results may differ from a plain program's by a relative error of at most 0.001.
Values may be sent and summed in bfloat16 or wider, within the bound.
A program may use at most 128 MiB of HBM per device.

v0:
```python
import jax
import jax.numpy as jnp
from jax import lax
from jax.sharding import PartitionSpec as P

REACH = 8
OWNER_SLOT_LIMIT = 2
CAP = 16


def from_behind(block, axis, distance):
    devices = range(lax.axis_size(axis))
    route = [((i - distance) % len(devices), i) for i in devices]
    return lax.ppermute(block, axis, route)


def per_device(key_values, bases, owner_slots):
    dev_count = lax.axis_size("seq")
    layers = key_values.shape[0]
    width = bases.shape[2]
    rank = bases.shape[3]
    tok_dev = key_values.shape[2] // dev_count
    tokens = tok_dev * dev_count
    blk_dev = owner_slots.shape[1]
    blk_rows = tok_dev // blk_dev
    whole = lax.all_to_all(key_values, "seq", split_axis=2, concat_axis=1, tiled=True)
    gram_list = []
    energy_list = []
    block_list = []
    for layer_idx in range(layers):
        slab_rows = whole[layer_idx]
        slab_rows = slab_rows.reshape(2, width, tok_dev)
        basis = bases[layer_idx]
        coeff = jnp.einsum(
            "scr,sct->srt", basis, slab_rows, preferred_element_type=jnp.float32
        ).astype(jnp.bfloat16)
        recon = jnp.einsum("scr,srt->sct", basis, coeff, preferred_element_type=jnp.float32)
        resid = slab_rows.astype(jnp.float32) - recon
        energy_term = jnp.sum(resid * resid, axis=2)
        gram_term = jnp.einsum("srt,sqt->srq", coeff, coeff, preferred_element_type=jnp.float32)
        gram_total, energy_total = lax.psum((gram_term, energy_term), "seq")
        gram_list.append(gram_total / tokens)
        energy_list.append(energy_total / tokens)
        block_list.append(coeff.reshape(2 * rank, blk_dev, blk_rows).transpose(1, 0, 2))
    grams = jnp.stack(gram_list)
    energies = jnp.stack(energy_list)
    unit_count = layers * blk_dev
    units = jnp.stack(block_list).reshape(unit_count, 2 * rank * blk_rows)
    slot_vals = owner_slots.reshape(unit_count)
    one_hot = (slot_vals[:, None] == jnp.arange(CAP, dtype=jnp.int32)[None, :]).astype(jnp.bfloat16)
    outgoing = jnp.einsum("us,uf->sf", one_hot, units, preferred_element_type=jnp.float32).astype(
        jnp.bfloat16
    )
    outgoing = outgoing.reshape(REACH, OWNER_SLOT_LIMIT, 2 * rank, blk_rows)
    arrived = [outgoing[0]]
    for offset in range(1, REACH):
        arrived.append(from_behind(outgoing[offset], "seq", offset))
    buffer_all = jnp.stack(arrived)
    received = buffer_all.reshape(REACH * OWNER_SLOT_LIMIT, 2 * rank, blk_rows)
    return (received, grams, energies)


def solution(mesh):
    in_specs = (P(None, "seq", "groups"), P(), P(None, ("groups", "seq")))
    out_specs = (
        P(("groups", "seq"), None, None),
        P("groups", None, None, None),
        P("groups", None, None),
    )
    return jax.shard_map(
        per_device, mesh=mesh, in_specs=in_specs, out_specs=out_specs, check_vma=False
    )
```

profile of v0, /device:TPU:0, one launch (start us, length us, event | category | flops | bytes accessed | tf_op | source)
XLA Modules:
  0.0 329.7 jit_solution(11468838820563559150)
XLA Ops:
  7.2 7.2 %copy.39 = bf16[3,128,4096]{1,0,2:T(4,128)(2,1)} copy(bf16[3,128,4096]{2,1,0:T(8,128)(2,1)} %param.3) | data formatting | bytes 6291456 | tf_op args[0]
  14.4 0.0 copy-start.3
  14.4 7.5 %all-to-all-start = ((bf16[3,128,4096]{1,0,2:T(4,128)(2,1)}), bf16[3,128,4096]{1,0,2:T(4,128)(2,1)}, u32[]{:S(2)}, u32[]{:S(2)}) async-start(bf16[3,128,4096]{1,0,2:T(4,128)(2,1)} %copy.39), calls=%async_computation | async-start | bytes 8388608 | tf_op jit(solution)/shard_map/all_to_all | solution.py:26
  22.0 0.0 all-reduce.4.cloned.1.call-start
  22.0 0.0 copy-done.3
  22.0 0.1 copy.37
  22.1 0.1 eq.15
  22.2 77.4 %all-to-all-done = bf16[3,128,4096]{1,0,2:T(4,128)(2,1)} async-done(((bf16[3,128,4096]{1,0,2:T(4,128)(2,1)}), bf16[3,128,4096]{1,0,2:T(4,128)(2,1)}, u32[]{:S(2)}, u32[]{:S(2)}) %all-to-all-start) | async-done | bytes 3145760 | tf_op jit(solution)/shard_map/all_to_all | solution.py:26
  99.6 5.5 %copy.40 = bf16[3,128,16,256]{3,1,2,0:T(8,128)(2,1)S(1)} copy(bf16[3,128,16,256]{1,0,3,2:T(4,128)(2,1)} %bitcast.1) | data formatting | bytes 6291456 | tf_op jit(solution)/shard_map/all_to_all | solution.py:26
  105.1 0.0 copy-start.4
  105.2 1.6 fusion.21
  106.8 1.0 copy-done.4
  107.8 0.5 convolution_convert_fusion.2
  108.3 0.0 copy-start.1
  108.3 0.6 fusion.3
  108.9 0.1 reshape.45
  109.0 0.0 copy-start.2
  109.0 0.6 copy-done.1
  109.5 1.8 convolution_convert_fusion.1
  111.3 0.0 copy-done.2
  111.3 0.0 copy-start
  111.3 1.9 fusion.1
  113.2 0.1 reshape.46
  113.3 0.0 copy-done
  113.3 1.7 convolution_convert_fusion.3
  115.0 1.8 fusion.5
  116.8 0.1 reshape.44
  116.9 1.1 fusion.22
  118.0 1.1 fusion.23
  119.0 1.1 fusion.24
  120.1 0.1 copy_bitcast_fusion.7
  120.2 0.1 pad_maximum_fusion.1
  120.3 0.9 convolution_convert_fusion
  121.2 1.5 slice_bitcast_fusion
  122.8 0.7 bitcast_dynamic-update-slice_fusion
  123.5 0.8 collective-permute-start
  124.4 6.2 %collective-permute-start.1 = (bf16[2,512,128]{2,1,0:T(8,128)(2,1)S(1)}, bf16[2,512,128]{2,1,0:T(8,128)(2,1)S(1)}, u32[]{:S(2)}, u32[]{:S(2)}) collective-permute-start(bf16[2,512,128]{2,1,0:T(8,128)(2,1)S(1)} %bitcast.153), channel_id=1, source_target_pairs={{14,0},{15,1},{0,2},{1,3},{2,4},{3,5},{4,6},{5,7},{6,8},{7,9},{8,1... | collective-permute-start | bytes 786440 | tf_op jit(solution)/shard_map/ppermute | solution.py:14
  130.7 12.0 %collective-permute-start.2 = (bf16[2,512,128]{2,1,0:T(8,128)(2,1)S(1)}, bf16[2,512,128]{2,1,0:T(8,128)(2,1)S(1)}, u32[]{:S(2)}, u32[]{:S(2)}) collective-permute-start(bf16[2,512,128]{2,1,0:T(8,128)(2,1)S(1)} %bitcast.152), channel_id=1, source_target_pairs={{13,0},{14,1},{15,2},{0,3},{1,4},{2,5},{3,6},{4,7},{5,8},{6,9},{7,... | collective-permute-start | bytes 786440 | tf_op jit(solution)/shard_map/ppermute | solution.py:14
  142.7 0.7 collective-permute-start.3
  143.5 0.2 collective-permute-start.4
  143.6 75.5 %all-reduce = (f32[2,1024]{1,0:T(2,128)S(1)}, f32[2,1024]{1,0:T(2,128)S(1)}, f32[2,1024]{1,0:T(2,128)S(1)}) all-reduce(f32[2,1024]{1,0:T(2,128)S(1)} %fusion.1, f32[2,1024]{1,0:T(2,128)S(1)} %fusion.3, f32[2,1024]{1,0:T(2,128)S(1)} %fusion.5), channel_id=1, replica_groups=mesh['groups'=2,'seq'=16] {'seq'}, use_global_device_ids=true, to_apply=%region_8.0 | all-reduce | flops 6144 | bytes 49152 | tf_op jit(solution)/shard_map/psum | solution.py:41
  219.1 0.6 pad_maximum_fusion.2
  219.9 0.0 all-reduce.4.cloned.1.call-update
  219.9 0.0 collective-permute-done
  219.9 0.1 collective-permute-start.5
  220.0 0.7 bitcast_dynamic-update-slice_fusion.7
  220.7 0.0 collective-permute-done.1
  220.7 0.0 collective-permute-start.6
  220.7 0.7 bitcast_dynamic-update-slice_fusion.6
  221.4 0.0 collective-permute-done.2
  221.4 0.7 bitcast_dynamic-update-slice_fusion.5
  222.1 0.0 collective-permute-done.3
  222.1 0.7 bitcast_dynamic-update-slice_fusion.4
  222.9 0.0 collective-permute-done.4
  222.9 0.7 bitcast_dynamic-update-slice_fusion.3
  223.6 16.2 %collective-permute-done.5 = bf16[2,512,128]{2,1,0:T(8,128)(2,1)S(1)} collective-permute-done((bf16[2,512,128]{2,1,0:T(8,128)(2,1)S(1)}, bf16[2,512,128]{2,1,0:T(8,128)(2,1)S(1)}, u32[]{:S(2)}, u32[]{:S(2)}) %collective-permute-start.5) | collective-permute-done | bytes 262176 | tf_op jit(solution)/shard_map/ppermute | solution.py:14
  239.8 0.7 bitcast_dynamic-update-slice_fusion.2
  240.5 0.0 collective-permute-done.6
  240.5 0.7 bitcast_dynamic-update-slice_fusion.1
  241.2 78.0 %all-reduce.4.cloned.1.call-done = (f32[2,256,256]{2,1,0:T(8,128)}, f32[2,256,256]{2,1,0:T(8,128)}, f32[2,256,256]{2,1,0:T(8,128)}) async-done(((f32[2,256,256]{2,1,0:T(8,128)}, f32[2,256,256]{2,1,0:T(8,128)}, f32[2,256,256]{2,1,0:T(8,128)}), (f32[2,256,256]{2,1,0:T(8,128)}, f32[2,256,256]{2,1,0:T(8,128)}, f32[2,256,256]{2,1,0:T(8,128)})) %all-reduce.4.cloned.1.call-update) | async-done | bytes 1572880 | tf_op jit(solution)/shard_map/psum | solution.py:41
  319.2 1.1 multiply_bitcast_fusion.2
  320.3 1.3 multiply_bitcast_fusion
  321.6 1.2 pad_maximum_fusion
  (10 shorter events, 0.3 us)
Async XLA Ops:
  14.4 7.6 %copy-start.3 = (s32[3,2]{0,1:T(2,128)S(1)}, s32[3,2]{0,1:T(2,128)}, u32[]{:S(2)}) copy-start(s32[3,2]{0,1:T(2,128)} %param.5) | copy-start | bytes 76
  14.4 85.2 %all-to-all-start = ((bf16[3,128,4096]{1,0,2:T(4,128)(2,1)}), bf16[3,128,4096]{1,0,2:T(4,128)(2,1)}, u32[]{:S(2)}, u32[]{:S(2)}) async-start(bf16[3,128,4096]{1,0,2:T(4,128)(2,1)} %copy.39), calls=%async_computation | async-start | bytes 8388608 | tf_op jit(solution)/shard_map/all_to_all | solution.py:26
  22.0 297.3 %all-reduce.4.cloned.1.call-start = ((), (), s32[]{:S(2)}) async-start(), calls=%async_computation.1 | async-start | bytes 3145728 | tf_op jit(solution)/shard_map/psum | solution.py:41
  105.1 2.6 copy-start.4
  108.3 1.2 copy-start.1
  109.0 2.3 copy-start.2
  111.3 2.0 copy-start
  123.5 96.4 %collective-permute-start = (bf16[2,512,128]{2,1,0:T(8,128)(2,1)S(1)}, bf16[2,512,128]{2,1,0:T(8,128)(2,1)S(1)}, u32[]{:S(2)}, u32[]{:S(2)}) collective-permute-start(bf16[2,512,128]{2,1,0:T(8,128)(2,1)S(1)} %bitcast.154), channel_id=1, source_target_pairs={{15,0},{0,1},{1,2},{2,3},{3,4},{4,5},{5,6},{6,7},{7,8},{8,9},{9,10... | collective-permute-start | bytes 786440 | tf_op jit(solution)/shard_map/ppermute | solution.py:14
  124.4 96.3 %collective-permute-start.1 = (bf16[2,512,128]{2,1,0:T(8,128)(2,1)S(1)}, bf16[2,512,128]{2,1,0:T(8,128)(2,1)S(1)}, u32[]{:S(2)}, u32[]{:S(2)}) collective-permute-start(bf16[2,512,128]{2,1,0:T(8,128)(2,1)S(1)} %bitcast.153), channel_id=1, source_target_pairs={{14,0},{15,1},{0,2},{1,3},{2,4},{3,5},{4,6},{5,7},{6,8},{7,9},{8,1... | collective-permute-start | bytes 786440 | tf_op jit(solution)/shard_map/ppermute | solution.py:14
  130.7 90.7 %collective-permute-start.2 = (bf16[2,512,128]{2,1,0:T(8,128)(2,1)S(1)}, bf16[2,512,128]{2,1,0:T(8,128)(2,1)S(1)}, u32[]{:S(2)}, u32[]{:S(2)}) collective-permute-start(bf16[2,512,128]{2,1,0:T(8,128)(2,1)S(1)} %bitcast.152), channel_id=1, source_target_pairs={{13,0},{14,1},{15,2},{0,3},{1,4},{2,5},{3,6},{4,7},{5,8},{6,9},{7,... | collective-permute-start | bytes 786440 | tf_op jit(solution)/shard_map/ppermute | solution.py:14
  142.7 79.4 %collective-permute-start.3 = (bf16[2,512,128]{2,1,0:T(8,128)(2,1)S(1)}, bf16[2,512,128]{2,1,0:T(8,128)(2,1)S(1)}, u32[]{:S(2)}, u32[]{:S(2)}) collective-permute-start(bf16[2,512,128]{2,1,0:T(8,128)(2,1)S(1)} %bitcast.151), channel_id=1, source_target_pairs={{12,0},{13,1},{14,2},{15,3},{0,4},{1,5},{2,6},{3,7},{4,8},{5,9},{6... | collective-permute-start | bytes 786440 | tf_op jit(solution)/shard_map/ppermute | solution.py:14
  143.5 79.4 %collective-permute-start.4 = (bf16[2,512,128]{2,1,0:T(8,128)(2,1)S(1)}, bf16[2,512,128]{2,1,0:T(8,128)(2,1)S(1)}, u32[]{:S(2)}, u32[]{:S(2)}) collective-permute-start(bf16[2,512,128]{2,1,0:T(8,128)(2,1)S(1)} %bitcast.150), channel_id=1, source_target_pairs={{11,0},{12,1},{13,2},{14,3},{15,4},{0,5},{1,6},{2,7},{3,8},{4,9},{... | collective-permute-start | bytes 786440 | tf_op jit(solution)/shard_map/ppermute | solution.py:14
  219.9 19.9 %collective-permute-start.5 = (bf16[2,512,128]{2,1,0:T(8,128)(2,1)S(1)}, bf16[2,512,128]{2,1,0:T(8,128)(2,1)S(1)}, u32[]{:S(2)}, u32[]{:S(2)}) collective-permute-start(bf16[2,512,128]{2,1,0:T(8,128)(2,1)S(1)} %bitcast.156), channel_id=1, source_target_pairs={{10,0},{11,1},{12,2},{13,3},{14,4},{15,5},{0,6},{1,7},{2,8},{3,9},... | collective-permute-start | bytes 786440 | tf_op jit(solution)/shard_map/ppermute | solution.py:14
  220.7 19.8 %collective-permute-start.6 = (bf16[2,512,128]{2,1,0:T(8,128)(2,1)S(1)}, bf16[2,512,128]{2,1,0:T(8,128)(2,1)S(1)}, u32[]{:S(2)}, u32[]{:S(2)}) collective-permute-start(bf16[2,512,128]{2,1,0:T(8,128)(2,1)S(1)} %bitcast.155), channel_id=1, source_target_pairs={{9,0},{10,1},{11,2},{12,3},{13,4},{14,5},{15,6},{0,7},{1,8},{2,9},... | collective-permute-start | bytes 786440 | tf_op jit(solution)/shard_map/ppermute | solution.py:14
Sparse Core Ops, SparseCore 0:
  220.0 99.1 all-reduce.3
where the time goes:
time: 330 us
  waiting for transfers between devices  172 us (52%)
  blocking collectives  75.5 us (23%)
  starting transfers between devices  27.6 us (8%)
  local copies, waits for them, and re-layouts  24 us (7%)
  between operations  14.3 us (4%)
  matrix products  12.3 us (4%)
  other arithmetic  4.34 us (1%)
    psum x1, waiting for transfers between devices, per_device(): gram_total, energy_total = lax.psum((gram_term, energy_term), 'seq')  78 us
    all_to_all x1, waiting for transfers between devices, per_device(): lax.all_to_all(key_values, 'seq', split_axis=2, concat_axis=1, tiled=True)  77.4 us
    psum x1, blocking collectives, per_device(): gram_total, energy_total = lax.psum((gram_term, energy_term), 'seq')  75.5 us
    ppermute x7, starting transfers between devices, from_behind(): return lax.ppermute(block, axis, route)  20 us
    ppermute x7, waiting for transfers between devices, from_behind(): return lax.ppermute(block, axis, route)  16.2 us
    unnamed x27, local copies, waits for them, and re-layouts  15.8 us
    all_to_all x1, starting transfers between devices, per_device(): lax.all_to_all(key_values, 'seq', split_axis=2, concat_axis=1, tiled=True)  7.54 us
  transfers between devices with their start and end apart: 9, of which 3 were waited for; matrix products, arithmetic and copies ran while one was open for 2% of the time, Pallas kernels for 0%

commit v1 on v0

--- a/solution.py
+++ b/solution.py
@@ -6,6 +6,12 @@
 REACH = 8
 OWNER_SLOT_LIMIT = 2
 CAP = 16
+
+
+def stacked_exchange(array, axis, split, join):
+    parts = jnp.split(array, lax.axis_size(axis), axis=split)
+    arrived = lax.all_to_all(jnp.stack(parts), axis, 0, 0)
+    return jnp.concatenate(arrived, axis=join)
 
 
 def from_behind(block, axis, distance):
@@ -23,7 +29,7 @@
     tokens = tok_dev * dev_count
     blk_dev = owner_slots.shape[1]
     blk_rows = tok_dev // blk_dev
-    whole = lax.all_to_all(key_values, "seq", split_axis=2, concat_axis=1, tiled=True)
+    whole = stacked_exchange(key_values, "seq", 2, 1)
     gram_list = []
     energy_list = []
     block_list = []

time: 330 us -> 327 us (level)
  waiting for transfers between devices: 172 us -> 154 us
  local copies, waits for them, and re-layouts: 24 us -> 38.7 us
  starting transfers between devices: 27.6 us -> 23.3 us
    all_to_all x1, waiting for transfers between devices: 77.4 us -> 59.1 us  [stacked_exchange(): arrived = lax.all_to_all(jnp.stack(parts), axis, 0, 0)]
    unnamed x27 -> x37, local copies, waits for them, and re-layouts: 15.8 us -> 31.2 us
    another operation x0 -> x4, local copies, waits for them, and re-layouts: none -> 5.57 us  [the longest x3 3.94 us: per_device(): slab_rows = slab_rows.reshape(2, width, tok_dev)]
    all_to_all x1, local copies, waits for them, and re-layouts: 5.5 us -> 0.2 us  [stacked_exchange(): arrived = lax.all_to_all(jnp.stack(parts), axis, 0, 0)]
    ppermute x7, starting transfers between devices: 20 us -> 15.8 us  [from_behind(): return lax.ppermute(block, axis, route)]
where the time goes in v1:
time: 327 us; the launch traced here: 326 us
  waiting for transfers between devices  154 us (47%)
  blocking collectives  75.5 us (23%)
  local copies, waits for them, and re-layouts  38.7 us (12%)
  starting transfers between devices  23.3 us (7%)
  matrix products  14.9 us (5%)
  between operations  14.3 us (4%)
  other arithmetic  5.55 us (2%)
    psum x1, waiting for transfers between devices, per_device(): gram_total, energy_total = lax.psum((gram_term, energy_term), 'seq')  78.5 us
    psum x1, blocking collectives, per_device(): gram_total, energy_total = lax.psum((gram_term, energy_term), 'seq')  75.5 us
    all_to_all x1, waiting for transfers between devices, stacked_exchange(): arrived = lax.all_to_all(jnp.stack(parts), axis, 0, 0)  59.1 us
    unnamed x37, local copies, waits for them, and re-layouts  31.2 us
    ppermute x7, waiting for transfers between devices, from_behind(): return lax.ppermute(block, axis, route)  16.2 us
    ppermute x7, starting transfers between devices, from_behind(): return lax.ppermute(block, axis, route)  15.8 us
    all_to_all x1, starting transfers between devices, stacked_exchange(): arrived = lax.all_to_all(jnp.stack(parts), axis, 0, 0)  7.49 us
  transfers between devices with their start and end apart: 9, of which 3 were waited for; matrix products, arithmetic and copies ran while one was open for 2% of the time, Pallas kernels for 0%

profile of v1, /device:TPU:0, one launch (start us, length us, event | category | flops | bytes accessed | tf_op | source)
XLA Modules:
  0.0 326.0 jit_solution(17006212149676294502)
XLA Ops:
  7.2 1.6 bitcast_dynamic-update-slice_fusion.23
  8.8 1.6 bitcast_dynamic-update-slice_fusion.22
  10.4 1.6 bitcast_dynamic-update-slice_fusion.21
  12.0 1.6 bitcast_dynamic-update-slice_fusion.20
  13.6 1.6 bitcast_dynamic-update-slice_fusion.19
  15.2 1.6 bitcast_dynamic-update-slice_fusion.18
  16.8 1.6 bitcast_dynamic-update-slice_fusion.17
  18.5 1.6 bitcast_dynamic-update-slice_fusion.16
  20.1 1.6 bitcast_dynamic-update-slice_fusion.15
  21.7 1.6 bitcast_dynamic-update-slice_fusion.14
  23.3 1.6 bitcast_dynamic-update-slice_fusion.13
  24.9 1.6 bitcast_dynamic-update-slice_fusion.12
  26.6 1.6 bitcast_dynamic-update-slice_fusion.11
  28.2 1.6 bitcast_dynamic-update-slice_fusion.10
  29.8 1.6 bitcast_dynamic-update-slice_fusion.9
  31.4 1.6 bitcast_dynamic-update-slice_fusion.8
  33.0 7.5 %all-to-all-start = ((bf16[16,3,128,256]{3,2,1,0:T(8,128)(2,1)}), bf16[16,3,128,256]{3,2,1,0:T(8,128)(2,1)S(1)}, u32[]{:S(2)}, u32[]{:S(2)}) async-start(bf16[16,3,128,256]{3,2,1,0:T(8,128)(2,1)} %bitcast_dynamic-update-slice_fusion.8), calls=%async_computation | async-start | bytes 6291456 | tf_op jit(solution)/shard_map/all_to_all | solution.py:13
  40.6 0.1 copy.24
  40.7 0.1 eq.15
  40.8 59.1 %all-to-all-done = bf16[16,3,128,256]{3,2,1,0:T(8,128)(2,1)S(1)} async-done(((bf16[16,3,128,256]{3,2,1,0:T(8,128)(2,1)}), bf16[16,3,128,256]{3,2,1,0:T(8,128)(2,1)S(1)}, u32[]{:S(2)}, u32[]{:S(2)}) %all-to-all-start) | async-done | bytes 3145760 | tf_op jit(solution)/shard_map/all_to_all | solution.py:13
  99.9 0.2 copy.67
  100.1 0.2 fusion.21
  100.3 1.3 copy.36
  101.6 1.7 convolution_convert_fusion.3
  103.4 1.7 convolution_convert_fusion.2
  105.1 1.3 copy.37
  106.4 1.7 convolution_convert_fusion.1
  108.2 1.3 copy.38
  109.5 1.1 fusion.22
  110.6 2.0 fusion.5
  112.7 1.1 fusion.23
  113.7 1.7 fusion.3
  115.5 1.1 fusion.24
  116.6 1.7 fusion.1
  118.3 0.1 copy.27
  118.4 0.1 reshape.49
  118.5 0.1 copy.29
  118.6 0.1 reshape.50
  118.7 0.1 copy.31
  118.9 0.1 reshape.51
  118.9 1.3 pad_maximum_fusion.1
  120.2 0.1 copy.32
  120.4 0.9 convolution_convert_fusion
  121.3 1.5 slice_bitcast_fusion
  122.8 0.7 bitcast_dynamic-update-slice_fusion
  123.6 0.8 collective-permute-start
  124.4 4.8 %collective-permute-start.1 = (bf16[2,512,128]{2,1,0:T(8,128)(2,1)S(1)}, bf16[2,512,128]{2,1,0:T(8,128)(2,1)S(1)}, u32[]{:S(2)}, u32[]{:S(2)}) collective-permute-start(bf16[2,512,128]{2,1,0:T(8,128)(2,1)S(1)} %bitcast.184), channel_id=1, source_target_pairs={{14,0},{15,1},{0,2},{1,3},{2,4},{3,5},{4,6},{5,7},{6,8},{7,9},{8,1... | collective-permute-start | bytes 786440 | tf_op jit(solution)/shard_map/ppermute | solution.py:20
  129.3 9.2 %collective-permute-start.2 = (bf16[2,512,128]{2,1,0:T(8,128)(2,1)S(1)}, bf16[2,512,128]{2,1,0:T(8,128)(2,1)S(1)}, u32[]{:S(2)}, u32[]{:S(2)}) collective-permute-start(bf16[2,512,128]{2,1,0:T(8,128)(2,1)S(1)} %bitcast.183), channel_id=1, source_target_pairs={{13,0},{14,1},{15,2},{0,3},{1,4},{2,5},{3,6},{4,7},{5,8},{6,9},{7,... | collective-permute-start | bytes 786440 | tf_op jit(solution)/shard_map/ppermute | solution.py:20
  138.5 0.7 collective-permute-start.3
  139.3 0.2 collective-permute-start.4
  139.5 75.5 %all-reduce = (f32[2,1024]{1,0:T(2,128)S(1)}, f32[2,1024]{1,0:T(2,128)S(1)}, f32[2,1024]{1,0:T(2,128)S(1)}) all-reduce(f32[2,1024]{1,0:T(2,128)S(1)} %fusion.1, f32[2,1024]{1,0:T(2,128)S(1)} %fusion.3, f32[2,1024]{1,0:T(2,128)S(1)} %fusion.5), channel_id=1, replica_groups=mesh['groups'=2,'seq'=16] {'seq'}, use_global_device_ids=true, to_apply=%region_8.0 | all-reduce | flops 6144 | bytes 49152 | tf_op jit(solution)/shard_map/psum | solution.py:47
  215.0 0.6 pad_maximum_fusion.2
  215.8 0.7 bitcast_dynamic-update-slice_fusion.7
  216.5 0.7 bitcast_dynamic-update-slice_fusion.6
  217.2 0.7 bitcast_dynamic-update-slice_fusion.5
  218.0 0.7 bitcast_dynamic-update-slice_fusion.4
  218.7 0.7 bitcast_dynamic-update-slice_fusion.3
  219.4 16.1 %collective-permute-done.5 = bf16[2,512,128]{2,1,0:T(8,128)(2,1)S(1)} collective-permute-done((bf16[2,512,128]{2,1,0:T(8,128)(2,1)S(1)}, bf16[2,512,128]{2,1,0:T(8,128)(2,1)S(1)}, u32[]{:S(2)}, u32[]{:S(2)}) %collective-permute-start.5) | collective-permute-done | bytes 262176 | tf_op jit(solution)/shard_map/ppermute | solution.py:20
  235.6 0.7 bitcast_dynamic-update-slice_fusion.2
  236.3 0.7 bitcast_dynamic-update-slice_fusion.1
  237.0 78.5 %all-reduce.4.cloned.1.call-done = (f32[2,256,256]{2,1,0:T(8,128)}, f32[2,256,256]{2,1,0:T(8,128)}, f32[2,256,256]{2,1,0:T(8,128)}) async-done(((f32[2,256,256]{2,1,0:T(8,128)}, f32[2,256,256]{2,1,0:T(8,128)}, f32[2,256,256]{2,1,0:T(8,128)}), (f32[2,256,256]{2,1,0:T(8,128)}, f32[2,256,256]{2,1,0:T(8,128)}, f32[2,256,256]{2,1,0:T(8,128)})) %all-reduce.4.cloned.1.call-update) | async-done | bytes 1572880 | tf_op jit(solution)/shard_map/psum | solution.py:47
  315.5 1.1 multiply_bitcast_fusion.2
  316.6 1.3 multiply_bitcast_fusion
  317.9 1.2 pad_maximum_fusion
  (25 shorter events, 0.4 us)
Async XLA Ops:
  33.0 7.5 %copy-start.2 = (s32[3,2]{0,1:T(2,128)S(1)}, s32[3,2]{0,1:T(2,128)}, u32[]{:S(2)}) copy-start(s32[3,2]{0,1:T(2,128)} %param.5) | copy-start | bytes 76
  33.0 66.9 %all-to-all-start = ((bf16[16,3,128,256]{3,2,1,0:T(8,128)(2,1)}), bf16[16,3,128,256]{3,2,1,0:T(8,128)(2,1)S(1)}, u32[]{:S(2)}, u32[]{:S(2)}) async-start(bf16[16,3,128,256]{3,2,1,0:T(8,128)(2,1)} %bitcast_dynamic-update-slice_fusion.8), calls=%async_computation | async-start | bytes 6291456 | tf_op jit(solution)/shard_map/all_to_all | solution.py:13
  40.5 275.0 %all-reduce.4.cloned.1.call-start = ((), (), s32[]{:S(2)}) async-start(), calls=%async_computation.1 | async-start | bytes 3145728 | tf_op jit(solution)/shard_map/psum | solution.py:47
  109.5 4.2 %copy-start.1 = (bf16[2,1024,256]{1,2,0:T(8,128)(2,1)S(1)}, bf16[2,1024,256]{1,2,0:T(8,128)(2,1)}, u32[]{:S(2)}) copy-start(bf16[2,1024,256]{1,2,0:T(8,128)(2,1)} %copy.37) | copy-start | bytes 3145732
  112.6 3.9 %copy-start = (bf16[2,1024,256]{1,2,0:T(8,128)(2,1)S(1)}, bf16[2,1024,256]{1,2,0:T(8,128)(2,1)}, u32[]{:S(2)}) copy-start(bf16[2,1024,256]{1,2,0:T(8,128)(2,1)} %copy.38) | copy-start | bytes 3145732
  123.6 92.1 %collective-permute-start = (bf16[2,512,128]{2,1,0:T(8,128)(2,1)S(1)}, bf16[2,512,128]{2,1,0:T(8,128)(2,1)S(1)}, u32[]{:S(2)}, u32[]{:S(2)}) collective-permute-start(bf16[2,512,128]{2,1,0:T(8,128)(2,1)S(1)} %bitcast.185), channel_id=1, source_target_pairs={{15,0},{0,1},{1,2},{2,3},{3,4},{4,5},{5,6},{6,7},{7,8},{8,9},{9,10... | collective-permute-start | bytes 786440 | tf_op jit(solution)/shard_map/ppermute | solution.py:20
  124.4 92.1 %collective-permute-start.1 = (bf16[2,512,128]{2,1,0:T(8,128)(2,1)S(1)}, bf16[2,512,128]{2,1,0:T(8,128)(2,1)S(1)}, u32[]{:S(2)}, u32[]{:S(2)}) collective-permute-start(bf16[2,512,128]{2,1,0:T(8,128)(2,1)S(1)} %bitcast.184), channel_id=1, source_target_pairs={{14,0},{15,1},{0,2},{1,3},{2,4},{3,5},{4,6},{5,7},{6,8},{7,9},{8,1... | collective-permute-start | bytes 786440 | tf_op jit(solution)/shard_map/ppermute | solution.py:20
  129.3 87.9 %collective-permute-start.2 = (bf16[2,512,128]{2,1,0:T(8,128)(2,1)S(1)}, bf16[2,512,128]{2,1,0:T(8,128)(2,1)S(1)}, u32[]{:S(2)}, u32[]{:S(2)}) collective-permute-start(bf16[2,512,128]{2,1,0:T(8,128)(2,1)S(1)} %bitcast.183), channel_id=1, source_target_pairs={{13,0},{14,1},{15,2},{0,3},{1,4},{2,5},{3,6},{4,7},{5,8},{6,9},{7,... | collective-permute-start | bytes 786440 | tf_op jit(solution)/shard_map/ppermute | solution.py:20
  138.5 79.4 %collective-permute-start.3 = (bf16[2,512,128]{2,1,0:T(8,128)(2,1)S(1)}, bf16[2,512,128]{2,1,0:T(8,128)(2,1)S(1)}, u32[]{:S(2)}, u32[]{:S(2)}) collective-permute-start(bf16[2,512,128]{2,1,0:T(8,128)(2,1)S(1)} %bitcast.182), channel_id=1, source_target_pairs={{12,0},{13,1},{14,2},{15,3},{0,4},{1,5},{2,6},{3,7},{4,8},{5,9},{6... | collective-permute-start | bytes 786440 | tf_op jit(solution)/shard_map/ppermute | solution.py:20
  139.3 79.4 %collective-permute-start.4 = (bf16[2,512,128]{2,1,0:T(8,128)(2,1)S(1)}, bf16[2,512,128]{2,1,0:T(8,128)(2,1)S(1)}, u32[]{:S(2)}, u32[]{:S(2)}) collective-permute-start(bf16[2,512,128]{2,1,0:T(8,128)(2,1)S(1)} %bitcast.181), channel_id=1, source_target_pairs={{11,0},{12,1},{13,2},{14,3},{15,4},{0,5},{1,6},{2,7},{3,8},{4,9},{... | collective-permute-start | bytes 786440 | tf_op jit(solution)/shard_map/ppermute | solution.py:20
  215.7 19.8 %collective-permute-start.5 = (bf16[2,512,128]{2,1,0:T(8,128)(2,1)S(1)}, bf16[2,512,128]{2,1,0:T(8,128)(2,1)S(1)}, u32[]{:S(2)}, u32[]{:S(2)}) collective-permute-start(bf16[2,512,128]{2,1,0:T(8,128)(2,1)S(1)} %bitcast.187), channel_id=1, source_target_pairs={{10,0},{11,1},{12,2},{13,3},{14,4},{15,5},{0,6},{1,7},{2,8},{3,9},... | collective-permute-start | bytes 786440 | tf_op jit(solution)/shard_map/ppermute | solution.py:20
  216.5 19.8 %collective-permute-start.6 = (bf16[2,512,128]{2,1,0:T(8,128)(2,1)S(1)}, bf16[2,512,128]{2,1,0:T(8,128)(2,1)S(1)}, u32[]{:S(2)}, u32[]{:S(2)}) collective-permute-start(bf16[2,512,128]{2,1,0:T(8,128)(2,1)S(1)} %bitcast.186), channel_id=1, source_target_pairs={{9,0},{10,1},{11,2},{12,3},{13,4},{14,5},{15,6},{0,7},{1,8},{2,9},... | collective-permute-start | bytes 786440 | tf_op jit(solution)/shard_map/ppermute | solution.py:20
Sparse Core Ops, SparseCore 0:
  215.8 99.6 all-reduce.3
